TPU v7x, 32 devices: a whole 2x2x4 slice. The times are simulated.
32 devices in a mesh: doc: 8 (over z, core), clu: 4 (over y, x).
Axes of the slice: x: 2, y: 2, z: 4, core: 2. Of those that a mesh axis runs over, the one named last changes fastest.
Arguments:
- embeddings: bfloat16 [4096, 256], P(('doc', 'clu')), may hold values from -16 to 16
- centroids: bfloat16 [4096, 256], P('clu'), may hold values from -1 to 1
Outputs:
- new_centroids: float32 [256, 4096], P('doc', 'clu')
- cluster_mass: float32 [4096], P('clu')
All inputs are finite; a program needn't handle non-finite values.
Results may differ from a plain program's by a relative error of at most 0.0011.
Values may be sent and summed in bfloat16 or wider, within the bound.
A program may use at most 64 MiB of HBM per device.

v0:
```python
import math

import jax
import jax.numpy as jnp
from jax import lax
from jax.sharding import PartitionSpec as P

K = 4096
ITERS = 2


entropic_smoothing = 0.05


def tile_scores(row_block, center_block):
    similarity_energy = lax.dot_general(
        row_block, center_block, (((1,), (1,)), ((), ())), preferred_element_type=jnp.float32
    )
    return similarity_energy / entropic_smoothing


def split_rows(portion, extra):
    row_count = portion.shape[0]
    block_size = math.gcd(row_count, 512)
    block_count = row_count // block_size
    return (
        portion.reshape(block_count, block_size, portion.shape[1]),
        extra.reshape(block_count, block_size),
    )


def local(embeddings, centroids):
    features = embeddings.shape[1]
    local_rows = embeddings.shape[0]
    own_cols = centroids.shape[0]
    doc_total = local_rows * lax.axis_size("doc") * lax.axis_size("clu")
    block_rows = local_rows * lax.axis_size("clu")
    log_docs = jnp.log(jnp.float32(doc_total))
    log_clusters = jnp.log(jnp.float32(K))
    potential = jnp.zeros((block_rows,), jnp.float32)
    col_pot = jnp.zeros((own_cols,), jnp.float32)
    for iteration in range(ITERS):
        start_state = (
            jnp.full((own_cols,), -jnp.inf, jnp.float32),
            jnp.zeros((own_cols,), jnp.float32),
        )
        column_row_pot = potential
        column_blocks, column_dual_variable_tiles = split_rows(
            lax.all_gather(embeddings, "clu", axis=0, tiled=True), column_row_pot
        )

        def column_per_block(state, inputs):
            similarity_energy = tile_scores(inputs[0], centroids) + inputs[1][:, None]
            highest = jnp.maximum(state[0], jnp.max(similarity_energy, axis=0))
            expsum = state[1] * jnp.exp(state[0] - highest) + jnp.sum(
                jnp.exp(similarity_energy - highest[None, :]), axis=0
            )
            return ((highest, expsum), None)

        column_result, column_unused = lax.scan(
            column_per_block, start_state, (column_blocks, column_dual_variable_tiles)
        )
        highest, expsum = column_result
        grand_aggregate = lax.pmax(highest, "doc")
        expsum = lax.psum(expsum * jnp.exp(highest - grand_aggregate), "doc")
        highest = grand_aggregate
        col_pot = -log_clusters - (highest + jnp.log(expsum))

        def row_piece(portion):
            row_count = portion.shape[0]
            blocks, unused_pot = split_rows(portion, jnp.zeros((row_count,), jnp.float32))

            def row_per_block(row_block):
                similarity_energy = tile_scores(row_block, centroids) + col_pot[None, :]
                highest = jnp.max(similarity_energy, axis=1)
                return (highest, jnp.sum(jnp.exp(similarity_energy - highest[:, None]), axis=1))

            highest, expsum = lax.map(row_per_block, blocks)
            return jnp.stack([highest.reshape(row_count), expsum.reshape(row_count)])

        statistics = row_piece(lax.all_gather(embeddings, "clu", axis=0, tiled=True))
        highest, expsum = (statistics[0], statistics[1])
        grand_aggregate = lax.pmax(highest, "clu")
        expsum = lax.psum(expsum * jnp.exp(highest - grand_aggregate), "clu")
        highest = grand_aggregate
        potential = -log_docs - (highest + jnp.log(expsum))
    start_state = (
        jnp.zeros((features, own_cols), jnp.float32),
        jnp.zeros((own_cols,), jnp.float32),
    )
    blocks, dual_variable_tiles = split_rows(
        lax.all_gather(embeddings, "clu", axis=0, tiled=True), potential
    )

    def plan_per_block(state, inputs):
        plan = jnp.exp(
            tile_scores(inputs[0], centroids) + inputs[1][:, None] + col_pot[None, :] + log_docs
        )
        mass_part = state[1] + jnp.sum(plan, axis=0)
        partial_sum = state[0] + lax.dot_general(
            inputs[0],
            plan.astype(jnp.bfloat16),
            (((0,), (0,)), ((), ())),
            preferred_element_type=jnp.float32,
        )
        return ((partial_sum, mass_part), None)

    result, unused = lax.scan(plan_per_block, start_state, (blocks, dual_variable_tiles))
    partial_sum, mass_part = result
    fraction_total = lax.psum_scatter(partial_sum, "doc", scatter_dimension=0, tiled=True)
    squares, column_marginal = lax.psum(
        (jnp.sum(fraction_total * fraction_total, axis=0), mass_part), "doc"
    )
    new_centroids = fraction_total * lax.rsqrt(squares / features + 1e-06)
    cluster_mass = column_marginal * (jnp.float32(K) / jnp.float32(doc_total))
    return (new_centroids, cluster_mass)


def solution(mesh):
    placed = (P(("doc", "clu"), None), P("clu", None))
    return jax.shard_map(
        local, mesh=mesh, in_specs=placed, out_specs=(P("doc", "clu"), P("clu")), check_vma=False
    )
```

profile of v0, /device:TPU:0, one launch (start us, length us, event | category | flops | bytes accessed | tf_op | source)
XLA Modules:
  0.0 169.6 jit_solution(4591019415259584235)
XLA Ops:
  7.2 0.0 copy-start
  7.2 0.0 reduce-scatter.4.cloned.1.call-start
  7.2 10.9 %all_gather.2 = bf16[512,256]{1,0:T(8,128)(2,1)S(1)} all-gather(bf16[128,256]{1,0:T(8,128)(2,1)} %param.2), channel_id=1, replica_groups=mesh['doc'=8,'clu'=4] {'clu'}, dimensions={0}, use_global_device_ids=true | all-gather | bytes 327680 | tf_op jit(solution)/shard_map/all_gather | solution.py:92
  18.1 0.0 copy-done
  18.1 0.5 fusion.7
  18.6 14.9 %pmax.28 = f32[1024]{0:T(1024)S(1)} all-reduce(f32[1024]{0:T(1024)S(1)} %get-tuple-element.72), channel_id=1, replica_groups=mesh['doc'=8,'clu'=4] {'doc'}, use_global_device_ids=true, to_apply=%region_1.2 | all-reduce | flops 1024 | bytes 8192 | tf_op jit(solution)/shard_map/pmax | solution.py:64
  33.5 0.3 exponential_reduce_fusion.3
  33.8 13.6 %psum.42 = f32[1024]{0:T(1024)S(1)} all-reduce(f32[1024]{0:T(1024)S(1)} %exponential_multiply_fusion.1), channel_id=1, replica_groups=mesh['doc'=8,'clu'=4] {'doc'}, use_global_device_ids=true, to_apply=%region_3.4 | all-reduce | flops 1024 | bytes 8192 | tf_op jit(solution)/shard_map/psum | solution.py:65
  47.4 0.2 add_reduce_fusion.2
  47.7 0.5 exponential_reduce_fusion.2
  48.2 8.9 %pmax.29 = f32[512]{0:T(512)S(1)} all-reduce(f32[512]{0:T(512)S(1)} %add_reduce_fusion.2), channel_id=1, replica_groups=mesh['doc'=8,'clu'=4] {'clu'}, use_global_device_ids=true, to_apply=%region_5.6 | all-reduce | flops 512 | bytes 4096 | tf_op jit(solution)/shard_map/pmax | solution.py:83
  57.1 8.4 %psum.43 = f32[512]{0:T(512)S(1)} all-reduce(f32[512]{0:T(512)S(1)} %exponential_multiply_fusion.3), channel_id=1, replica_groups=mesh['doc'=8,'clu'=4] {'clu'}, use_global_device_ids=true, to_apply=%region_7.8 | all-reduce | flops 512 | bytes 4096 | tf_op jit(solution)/shard_map/psum | solution.py:84
  65.5 0.2 add_reduce_fusion.1
  65.7 0.4 exponential_reduce_fusion.1
  66.1 13.6 %pmax.30 = f32[1024]{0:T(1024)S(1)} all-reduce(f32[1024]{0:T(1024)S(1)} %add_reduce_fusion.1), channel_id=1, replica_groups=mesh['doc'=8,'clu'=4] {'doc'}, use_global_device_ids=true, to_apply=%region_9.10 | all-reduce | flops 1024 | bytes 8192 | tf_op jit(solution)/shard_map/pmax | solution.py:64
  79.8 13.6 %psum.44 = f32[1024]{0:T(1024)S(1)} all-reduce(f32[1024]{0:T(1024)S(1)} %exponential_multiply_fusion), channel_id=1, replica_groups=mesh['doc'=8,'clu'=4] {'doc'}, use_global_device_ids=true, to_apply=%region_11.12 | all-reduce | flops 1024 | bytes 8192 | tf_op jit(solution)/shard_map/psum | solution.py:65
  93.4 0.2 add_reduce_fusion
  93.6 8.9 %pmax.31 = f32[512]{0:T(512)S(1)} all-reduce(f32[512]{0:T(512)S(1)} %add_reduce_fusion), channel_id=1, replica_groups=mesh['doc'=8,'clu'=4] {'clu'}, use_global_device_ids=true, to_apply=%region_13.14 | all-reduce | flops 512 | bytes 4096 | tf_op jit(solution)/shard_map/pmax | solution.py:83
  102.5 0.5 exponential_reduce_fusion
  103.0 8.5 %psum.45 = f32[512]{0:T(512)S(1)} all-reduce(f32[512]{0:T(512)S(1)} %exponential_multiply_fusion.2), channel_id=1, replica_groups=mesh['doc'=8,'clu'=4] {'clu'}, use_global_device_ids=true, to_apply=%region_15.16 | all-reduce | flops 512 | bytes 4096 | tf_op jit(solution)/shard_map/psum | solution.py:84
  111.5 1.7 %convolution_bitcast_fusion = f32[256,1024]{0,1:T(8,128)} fusion(bf16[512,256]{1,0:T(8,128)(2,1)S(1)} %all_gather.2, f32[512,1024]{1,0:T(8,128)S(1)} %get-tuple-element.73, f32[512]{0:T(512)S(1)} %add_subtract_fusion.2, f32[1024]{0:T(1024)S(1)} %add_subtract_fusion), kind=kOutput, calls=%fused_computation.11 | convolution fusion | flops 270532608 | bytes 3414016 | tf_op jit(solution)/shard_map/while/body/eval_jaxpr/dot_general | solution.py:100
  113.2 2.5 %copy.6 = f32[256,1024]{1,0:T(8,128)} copy(f32[256,1024]{0,1:T(8,128)} %convolution_bitcast_fusion) | data formatting | bytes 2097152
  115.8 0.0 reduce-scatter.4.cloned.1.call-update
  115.8 0.5 fusion
  116.3 29.5 %reduce-scatter.4.cloned.1.call-done = f32[32,1024]{1,0:T(8,128)} async-done(((f32[256,1024]{1,0:T(8,128)}), f32[32,1024]{1,0:T(8,128)}) %reduce-scatter.4.cloned.1.call-update) | async-done | bytes 131088
  145.9 1.1 copy.7
  147.0 0.2 multiply_reduce_fusion
  147.2 14.5 %all-reduce = (f32[1024]{0:T(1024)S(1)}, f32[1024]{0:T(1024)}) all-reduce(f32[1024]{0:T(1024)S(1)} %multiply_reduce_fusion, f32[1024]{0:T(1024)S(1)} %fusion), channel_id=1, replica_groups=mesh['doc'=8,'clu'=4] {'doc'}, use_global_device_ids=true, to_apply=%region_18.19 | all-reduce | flops 2048 | bytes 16384 | tf_op jit(solution)/shard_map/psum | solution.py:111
  161.7 0.2 broadcast_multiply_fusion
  161.9 0.8 copy.5
  (9 shorter events, 0.1 us)
Async XLA Ops:
  7.2 10.9 %copy-start = (bf16[1024,256]{1,0:T(8,128)(2,1)S(1)}, bf16[1024,256]{1,0:T(8,128)(2,1)}, u32[]{:S(2)}) copy-start(bf16[1024,256]{1,0:T(8,128)(2,1)} %param.3) | copy-start | bytes 1572868
  7.2 138.7 %reduce-scatter.4.cloned.1.call-start = ((), (), s32[]{:S(2)}) async-start(), calls=%async_computation.1 | async-start | bytes 1179648
Sparse Core Ops, SparseCore 0:
  115.9 29.8 reduce-scatter.3
where the time goes:
time: 170 us
  blocking collectives  116 us (68%)
  waiting for transfers between devices  29.6 us (17%)
  between operations  14.1 us (8%)
  local copies, waits for them, and re-layouts  4.49 us (3%)
  other arithmetic  3.4 us (2%)
  matrix products  2.19 us (1%)
    unnamed x2, waiting for transfers between devices  29.6 us
    pmax x2, blocking collectives, local(): grand_aggregate = lax.pmax(highest, 'doc')  28.5 us
    psum x2, blocking collectives, local(): expsum = lax.psum(expsum * jnp.exp(highest - grand_aggregate), 'doc')  27.2 us
    pmax x2, blocking collectives, local(): grand_aggregate = lax.pmax(highest, 'clu')  17.8 us
    psum x2, blocking collectives, local(): expsum = lax.psum(expsum * jnp.exp(highest - grand_aggregate), 'clu')  16.9 us
    psum x1, blocking collectives, local(): lax.psum((jnp.sum(fraction_total * fraction_total, axis=0), mass_part), '...  14.5 us
    all_gather x1, blocking collectives, local(): lax.all_gather(embeddings, 'clu', axis=0, tiled=True)  10.9 us
    unnamed x5, local copies, waits for them, and re-layouts  4.49 us
  transfers between devices with their start and end apart: 1, of which 1 were waited for; matrix products, arithmetic and copies ran while one was open for 0% of the time, Pallas kernels for 0%

commit v1 on v0

v1 whole, which is shorter than its diff:
```python
import functools
import math

import jax
import jax.numpy as jnp
from jax import lax
from jax.experimental import pallas as pl
from jax.experimental.pallas import tpu as pltpu
from jax.sharding import PartitionSpec as P

ITERS = 2
SMOOTHING = 0.05
LOG2E = math.log2(math.e)
MESH = pl.DeviceIdType.MESH
F32 = jnp.float32


def kernel(
    nd, nc,
    emb_ref, cent_ref, out_ref, mass_ref,
    emb_all, scores, plan, rpot, colbuf, rowbuf, massbuf, sqbuf, sums, rsbuf, tot, pairbuf,
    own_sem, emb_ss, emb_rs, fwd_ss, col_ss, col_rs, row_ss, row_rs,
    mass_ss, mass_rs, sq_ss, sq_rs, sum_ss, sum_rs, pair_ss, pair_rs,
):
    nz = nd // 2
    nb = 2 * nc
    rows, features = emb_ref.shape
    half = cent_ref.shape[0] // 2
    own_f = features // nd
    log_docs = math.log2(rows * nd * nc)
    log_clusters = math.log2(2 * half * nc)
    d = lax.axis_index("doc")
    c = lax.axis_index("clu")
    core = lax.rem(d, 2)
    z = lax.div(d, 2)
    partner = d + 1 - 2 * core
    me = core * nc + c

    def block_peer(k):
        peer = lax.rem(me + k, nb)
        return peer, (2 * z + lax.div(peer, nc), lax.rem(peer, nc))

    def z_peer(k):
        peer = lax.rem(z + k, nz)
        return peer, (2 * peer + core, c)

    def doc_peer(k):
        peer = lax.rem(d + k, nd)
        return peer, (peer, c)

    def remote(src, dst, ss, rs, device):
        return pltpu.make_async_remote_copy(
            src_ref=src, dst_ref=dst, send_sem=ss, recv_sem=rs,
            device_id=device, device_id_type=MESH,
        )

    sends = []

    def send(*args):
        copy = remote(*args)
        copy.start()
        sends.append(copy)

    barrier = pltpu.get_barrier_semaphore()
    for k in range(1, nb):
        pl.semaphore_signal(barrier, inc=1, device_id=block_peer(k)[1], device_id_type=MESH)
    for k in range(1, nd):
        pl.semaphore_signal(barrier, inc=1, device_id=doc_peer(k)[1], device_id_type=MESH)
    own_copy = pltpu.make_async_copy(emb_ref, emb_all.at[me], own_sem)
    own_copy.start()
    centers = cent_ref[pl.ds(pl.multiple_of(core * half, half), half), :]
    pl.semaphore_wait(barrier, nb - 1 + nd - 1)

    for k in range(1, nc):
        send(emb_ref, emb_all.at[me], emb_ss.at[k], emb_rs.at[me], (d, lax.rem(c + k, nc)))
    send(emb_ref, emb_all.at[me], emb_ss.at[0], emb_rs.at[me], (partner, c))

    def col_update(state, t):
        high, total = state
        t = t.reshape(rows // 8, 8, half)
        new = jnp.maximum(high, jnp.max(t, axis=0))
        total = total * jnp.exp2(high - new) + jnp.sum(jnp.exp2(t - new[None]), axis=0)
        return new, total

    state = (jnp.full((8, half), -jnp.inf, F32), jnp.zeros((8, half), F32))

    def first_block(state, slot):
        s = lax.dot_general(
            emb_all[slot], centers, (((1,), (1,)), ((), ())), preferred_element_type=F32
        ) * (LOG2E / SMOOTHING)
        scores[slot] = s
        return col_update(state, s)

    def arrive(slot):
        remote(
            emb_all.at[slot], emb_all.at[slot], emb_ss.at[0], emb_rs.at[slot], (partner, c)
        ).wait_recv()

    own_copy.wait()
    state = first_block(state, me)
    other = 1 - core
    for k in range(1, nc):
        slot = core * nc + lax.rem(c + k, nc)
        arrive(slot)
        send(emb_all.at[slot], emb_all.at[slot], fwd_ss.at[k], emb_rs.at[slot], (partner, c))
        state = first_block(state, slot)
    for k in range(nc):
        slot = other * nc + lax.rem(c + k, nc)
        arrive(slot)
        state = first_block(state, slot)

    diagonal = lax.broadcasted_iota(jnp.int32, (rows, rows), 0) == lax.broadcasted_iota(
        jnp.int32, (rows, rows), 1
    )

    def to_lanes(x):
        return jnp.sum(jnp.where(diagonal, x, 0.0), axis=0, keepdims=True)

    def to_sublanes(x):
        return jnp.sum(jnp.where(diagonal, x, 0.0), axis=1, keepdims=True)

    def column_potential(it, state):
        high, total = state
        top = jnp.max(high, axis=0, keepdims=True)
        colbuf[it, z, 0:1, :] = top
        colbuf[it, z, 1:2, :] = jnp.sum(total * jnp.exp2(high - top), axis=0, keepdims=True)
        mine = colbuf.at[it, z]
        for k in range(1, nz):
            send(mine, mine, col_ss.at[it, k], col_rs.at[it, z], z_peer(k)[1])
        for k in range(1, nz):
            peer, device = z_peer(k)
            theirs = colbuf.at[it, peer]
            remote(theirs, theirs, col_ss.at[it, k], col_rs.at[it, peer], device).wait_recv()
        tops = [colbuf[it, s, 0:1, :] for s in range(nz)]
        top = functools.reduce(jnp.maximum, tops)
        total = sum(colbuf[it, s, 1:2, :] * jnp.exp2(tops[s] - top) for s in range(nz))
        return -log_clusters - (top + jnp.log2(total))

    def row_potential(it, col_pot):
        def block(b, carry):
            t = scores[b] + col_pot
            high = jnp.max(t, axis=1, keepdims=True)
            total = jnp.sum(jnp.exp2(t - high), axis=1, keepdims=True)
            rowbuf[it, me, pl.ds(b, 1), :] = to_lanes(high)
            rowbuf[it, me, pl.ds(nb + b, 1), :] = to_lanes(total)
            return carry

        lax.fori_loop(0, nb, block, 0)
        mine = rowbuf.at[it, me]
        for k in range(1, nb):
            send(mine, mine, row_ss.at[it, k], row_rs.at[it, me], block_peer(k)[1])
        for k in range(1, nb):
            peer, device = block_peer(k)
            theirs = rowbuf.at[it, peer]
            remote(theirs, theirs, row_ss.at[it, k], row_rs.at[it, peer], device).wait_recv()
        high = rowbuf[it, :, 0:nb, :]
        top = jnp.max(high, axis=0)
        total = jnp.sum(rowbuf[it, :, nb:, :] * jnp.exp2(high - top[None]), axis=0)
        rpot[...] = -log_docs - (top + jnp.log2(total))

    for it in range(ITERS):
        if it > 0:
            def again(b, state):
                return col_update(state, scores[b] + to_sublanes(rpot[pl.ds(b, 1), :]))

            state = lax.fori_loop(
                0, nb, again,
                (jnp.full((8, half), -jnp.inf, F32), jnp.zeros((8, half), F32)),
            )
        col_pot = column_potential(it, state)
        row_potential(it, col_pot)

    def plan_block(b, mass):
        t = scores[b] + to_sublanes(rpot[pl.ds(b, 1), :]) + col_pot + log_docs
        p = jnp.exp2(t)
        plan[pl.ds(pl.multiple_of(b * rows, rows), rows), :] = p.astype(jnp.bfloat16)
        return mass + jnp.sum(p.reshape(rows // 8, 8, half), axis=0)

    mass = lax.fori_loop(0, nb, plan_block, jnp.zeros((8, half), F32))
    sums[...] = lax.dot_general(
        emb_all[...].reshape(nb * rows, features), plan[...],
        (((0,), (0,)), ((), ())), preferred_element_type=F32,
    )
    massbuf[d] = jnp.sum(mass, axis=0, keepdims=True)
    far = sorted(range(1, nz), key=lambda k: -min(k, nz - k))

    def share(peer):
        return sums.at[pl.ds(pl.multiple_of(peer * 2 * own_f, 2 * own_f), 2 * own_f), :]

    for k in far:
        peer, device = z_peer(k)
        send(share(peer), rsbuf.at[z], sum_ss.at[k], sum_rs.at[z], device)
    for k in range(1, nd):
        send(massbuf.at[d], massbuf.at[d], mass_ss.at[k], mass_rs.at[d], doc_peer(k)[1])
    total = share(z)[...]
    for k in reversed(far):
        peer, device = z_peer(k)
        remote(share(z), rsbuf.at[peer], sum_ss.at[k], sum_rs.at[peer], device).wait_recv()
        total = total + rsbuf[peer]
    tot[...] = total
    sqbuf[d] = jnp.sum(total * total, axis=0, keepdims=True)

    def features_of(which):
        return tot.at[pl.ds(pl.multiple_of(which * own_f, own_f), own_f), :]

    for k in range(1, nd):
        send(sqbuf.at[d], sqbuf.at[d], sq_ss.at[k], sq_rs.at[d], doc_peer(k)[1])
    send(features_of(other), pairbuf, pair_ss, pair_rs, (partner, c))
    for k in range(1, nd):
        peer, device = doc_peer(k)
        theirs = massbuf.at[peer]
        remote(theirs, theirs, mass_ss.at[k], mass_rs.at[peer], device).wait_recv()
        theirs = sqbuf.at[peer]
        remote(theirs, theirs, sq_ss.at[k], sq_rs.at[peer], device).wait_recv()
    remote(features_of(core), pairbuf, pair_ss, pair_rs, (partner, c)).wait_recv()

    def finish(which, block):
        columns = pl.ds(pl.multiple_of(which * half, half), half)
        squares = sum(sqbuf[2 * s + which] for s in range(nz))
        out_ref[:, columns] = block * lax.rsqrt(squares / features + 1e-06)
        mass_ref[:, columns] = sum(massbuf[2 * s + which] for s in range(nz)) * (
            2 * half * nc / (rows * nd * nc)
        )

    finish(core, features_of(core)[...])
    finish(other, pairbuf[...])
    for copy in sends:
        copy.wait_send()


def local(nd, nc, embeddings, centroids):
    rows, features = embeddings.shape
    own_cols = centroids.shape[0]
    half, nz, nb = own_cols // 2, nd // 2, 2 * nc
    own_f = features // nd
    dma = pltpu.SemaphoreType.DMA
    out, mass = pl.pallas_call(
        functools.partial(kernel, nd, nc),
        out_shape=(
            jax.ShapeDtypeStruct((own_f, own_cols), F32),
            jax.ShapeDtypeStruct((1, own_cols), F32),
        ),
        in_specs=[pl.BlockSpec(memory_space=pltpu.VMEM)] * 2,
        out_specs=(pl.BlockSpec(memory_space=pltpu.VMEM),) * 2,
        scratch_shapes=[
            pltpu.VMEM((nb, rows, features), jnp.bfloat16),
            pltpu.VMEM((nb, rows, half), F32),
            pltpu.VMEM((nb * rows, half), jnp.bfloat16),
            pltpu.VMEM((nb, rows), F32),
            pltpu.VMEM((ITERS, nz, 2, half), F32),
            pltpu.VMEM((ITERS, nb, 2 * nb, rows), F32),
            pltpu.VMEM((nd, 1, half), F32),
            pltpu.VMEM((nd, 1, half), F32),
            pltpu.VMEM((features, half), F32),
            pltpu.VMEM((nz, 2 * own_f, half), F32),
            pltpu.VMEM((2 * own_f, half), F32),
            pltpu.VMEM((own_f, half), F32),
            dma, dma((nc,)), dma((nb,)), dma((nc,)),
            dma((ITERS, nz)), dma((ITERS, nz)), dma((ITERS, nb)), dma((ITERS, nb)),
            dma((nd,)), dma((nd,)), dma((nd,)), dma((nd,)),
            dma((nz,)), dma((nz,)), dma, dma,
        ],
        compiler_params=pltpu.CompilerParams(
            collective_id=0, has_side_effects=True, vmem_limit_bytes=50 * 2**20
        ),
    )(embeddings, centroids)
    return out, mass.reshape(own_cols)


def solution(mesh):
    placed = (P(("doc", "clu"), None), P("clu", None))
    body = functools.partial(local, mesh.shape["doc"], mesh.shape["clu"])
    return jax.shard_map(
        body, mesh=mesh, in_specs=placed, out_specs=(P("doc", "clu"), P("clu")), check_vma=False
    )
```

time: 170 us -> 53.4 us (0.31)
  blocking collectives: 116 us -> 0 us
  Pallas kernels: 0 us -> 49.4 us
  waiting for transfers between devices: 29.6 us -> 0 us
  between operations: 14.1 us -> 0.65 us
  other arithmetic: 3.4 us -> 0 us
  matrix products: 2.19 us -> 0 us
    psum x5 -> x0, blocking collectives: 58.6 us -> none  [the longest x2 27.2 us: local(): expsum = lax.psum(expsum * jnp.exp(highest - grand_aggregate), 'doc')]
    pallas_call x0 -> x1, Pallas kernels: none -> 49.4 us  [local(): pl.pallas_call(functools.partial(kernel, nd, nc), out_shape=(jax.ShapeDty...]
    pmax x4 -> x0, blocking collectives: 46.3 us -> none  [the longest x2 28.5 us: local(): grand_aggregate = lax.pmax(highest, 'doc')]
    unnamed x2 -> x0, waiting for transfers between devices: 29.6 us -> none
    all_gather x1 -> x0, blocking collectives: 10.9 us -> none  [local(): lax.all_gather(embeddings, 'clu', axis=0, tiled=True)]
    reduce_sum x6 -> x0, other arithmetic: 2.46 us -> none  [the longest x2 1.02 us: row_per_block(): jnp.sum(jnp.exp(similarity_energy - highest[:, None]), axis=1)]
    dot_general x2 -> x0, matrix products: 2.19 us -> none  [the longest x1 1.72 us: plan_per_block(): lax.dot_general(inputs[0], plan.astype(jnp.bfloat16), (((0,), (0,)), ((),...]
    unnamed x5 -> x6, local copies, waits for them, and re-layouts: 4.49 us -> 3.12 us
  transfers between devices with their start and end apart: 1 -> 0, of which waited for: 1 -> 0; matrix products, arithmetic and copies ran while one was open for 0% -> 0% of each run, Pallas kernels for 0% -> 0%
where the time goes in v1:
time: 53.4 us; the launch traced here: 53.2 us
  Pallas kernels  49.4 us (93%)
  local copies, waits for them, and re-layouts  3.12 us (6%)
  between operations  0.65 us (1%)
    pallas_call x1, Pallas kernels, local(): pl.pallas_call(functools.partial(kernel, nd, nc), out_shape=(jax.ShapeDty...  49.4 us
    unnamed x6, local copies, waits for them, and re-layouts  3.12 us

profile of v1, /device:TPU:0, one launch (start us, length us, event | category | flops | bytes accessed | tf_op | source)
XLA Modules:
  0.0 53.2 jit_solution(17251031249921684845)
XLA Ops:
  0.6 0.0 copy-start
  0.6 1.0 %copy-done = bf16[1024,256]{1,0:T(8,128)(2,1)S(1)} copy-done((bf16[1024,256]{1,0:T(8,128)(2,1)S(1)}, bf16[1024,256]{1,0:T(8,128)(2,1)}, u32[]{:S(2)}) %copy-start) | copy-done | bytes 524312
  1.7 0.0 copy-start.1
  1.7 0.8 %copy-done.1 = bf16[128,256]{1,0:T(8,128)(2,1)S(1)} copy-done((bf16[128,256]{1,0:T(8,128)(2,1)S(1)}, bf16[128,256]{1,0:T(8,128)(2,1)}, u32[]{:S(2)}) %copy-start.1) | copy-done | bytes 65560
  2.5 49.4 %shard_map.41 = (f32[32,1024]{1,0:T(8,128)S(1)}, f32[1,1024]{1,0:T(1,128)S(1)}) custom-call(bf16[128,256]{1,0:T(8,128)(2,1)S(1)} %copy-done.1, bf16[1024,256]{1,0:T(8,128)(2,1)S(1)} %copy-done), custom_call_target="tpu_custom_call" | custom-call | tf_op jit(solution)/shard_map/pallas_call | solution.py:237
  51.9 0.7 %copy.6 = f32[32,1024]{1,0:T(8,128)} copy(f32[32,1024]{1,0:T(8,128)S(1)} %get-tuple-element.8) | data formatting | bytes 262144
  52.6 0.6 %copy.7 = f32[1024]{0:T(1024)} copy(f32[1024]{0:T(1024)S(1)} %bitcast.1) | data formatting | bytes 8192
Async XLA Ops:
  0.6 1.0 %copy-start = (bf16[1024,256]{1,0:T(8,128)(2,1)S(1)}, bf16[1024,256]{1,0:T(8,128)(2,1)}, u32[]{:S(2)}) copy-start(bf16[1024,256]{1,0:T(8,128)(2,1)} %cent_ref.1) | copy-start | bytes 1572868
  1.7 0.8 %copy-start.1 = (bf16[128,256]{1,0:T(8,128)(2,1)S(1)}, bf16[128,256]{1,0:T(8,128)(2,1)}, u32[]{:S(2)}) copy-start(bf16[128,256]{1,0:T(8,128)(2,1)} %emb_ref.1) | copy-start | bytes 196612

commit v2 on v1

--- a/solution.py
+++ b/solution.py
@@ -18,8 +18,8 @@
 def kernel(
     nd, nc,
     emb_ref, cent_ref, out_ref, mass_ref,
-    emb_all, scores, plan, rpot, colbuf, rowbuf, massbuf, sqbuf, sums, rsbuf, tot, pairbuf,
-    own_sem, emb_ss, emb_rs, fwd_ss, col_ss, col_rs, row_ss, row_rs,
+    emb_all, centers, scores, plan, rpot, colbuf, rowbuf, massbuf, sqbuf, sums, rsbuf, tot, pairbuf,
+    own_sem, cent_sem, emb_ss, emb_rs, fwd_ss, col_ss, col_rs, row_ss, row_rs,
     mass_ss, mass_rs, sq_ss, sq_rs, sum_ss, sum_rs, pair_ss, pair_rs,
 ):
     nz = nd // 2
@@ -61,19 +61,17 @@
         copy.start()
         sends.append(copy)
 
+    own_copy = pltpu.make_async_copy(emb_ref, emb_all.at[me], own_sem)
+    own_copy.start()
+    cent_copy = pltpu.make_async_copy(
+        cent_ref.at[pl.ds(pl.multiple_of(core * half, half), half), :], centers, cent_sem
+    )
+    cent_copy.start()
     barrier = pltpu.get_barrier_semaphore()
     for k in range(1, nb):
         pl.semaphore_signal(barrier, inc=1, device_id=block_peer(k)[1], device_id_type=MESH)
     for k in range(1, nd):
         pl.semaphore_signal(barrier, inc=1, device_id=doc_peer(k)[1], device_id_type=MESH)
-    own_copy = pltpu.make_async_copy(emb_ref, emb_all.at[me], own_sem)
-    own_copy.start()
-    centers = cent_ref[pl.ds(pl.multiple_of(core * half, half), half), :]
-    pl.semaphore_wait(barrier, nb - 1 + nd - 1)
-
-    for k in range(1, nc):
-        send(emb_ref, emb_all.at[me], emb_ss.at[k], emb_rs.at[me], (d, lax.rem(c + k, nc)))
-    send(emb_ref, emb_all.at[me], emb_ss.at[0], emb_rs.at[me], (partner, c))
 
     def col_update(state, t):
         high, total = state
@@ -86,7 +84,7 @@
 
     def first_block(state, slot):
         s = lax.dot_general(
-            emb_all[slot], centers, (((1,), (1,)), ((), ())), preferred_element_type=F32
+            emb_all[slot], centers[...], (((1,), (1,)), ((), ())), preferred_element_type=F32
         ) * (LOG2E / SMOOTHING)
         scores[slot] = s
         return col_update(state, s)
@@ -96,16 +94,29 @@
             emb_all.at[slot], emb_all.at[slot], emb_ss.at[0], emb_rs.at[slot], (partner, c)
         ).wait_recv()
 
+    def clu_peer(k):
+        if nc & (nc - 1):
+            return lax.rem(c + k, nc)
+        bits = [1 << i for i in range(nc.bit_length() - 1)]
+        return sum(lax.rem(lax.div(c, b) + k // b, 2) * b for b in bits)
+
     own_copy.wait()
+    cent_copy.wait()
     state = first_block(state, me)
+    pl.semaphore_wait(barrier, nb - 1 + nd - 1)
+
+    own = emb_all.at[me]
+    for k in reversed(range(1, nc)):
+        send(own, own, emb_ss.at[k], emb_rs.at[me], (d, clu_peer(k)))
+    send(own, own, emb_ss.at[0], emb_rs.at[me], (partner, c))
     other = 1 - core
     for k in range(1, nc):
-        slot = core * nc + lax.rem(c + k, nc)
+        slot = core * nc + clu_peer(k)
         arrive(slot)
         send(emb_all.at[slot], emb_all.at[slot], fwd_ss.at[k], emb_rs.at[slot], (partner, c))
         state = first_block(state, slot)
     for k in range(nc):
-        slot = other * nc + lax.rem(c + k, nc)
+        slot = other * nc + clu_peer(k)
         arrive(slot)
         state = first_block(state, slot)
 
@@ -122,8 +133,8 @@
     def column_potential(it, state):
         high, total = state
         top = jnp.max(high, axis=0, keepdims=True)
-        colbuf[it, z, 0:1, :] = top
-        colbuf[it, z, 1:2, :] = jnp.sum(total * jnp.exp2(high - top), axis=0, keepdims=True)
+        total = jnp.sum(total * jnp.exp2(high - top), axis=0, keepdims=True)
+        colbuf[it, z] = top + jnp.log2(total)
         mine = colbuf.at[it, z]
         for k in range(1, nz):
             send(mine, mine, col_ss.at[it, k], col_rs.at[it, z], z_peer(k)[1])
@@ -131,56 +142,66 @@
             peer, device = z_peer(k)
             theirs = colbuf.at[it, peer]
             remote(theirs, theirs, col_ss.at[it, k], col_rs.at[it, peer], device).wait_recv()
-        tops = [colbuf[it, s, 0:1, :] for s in range(nz)]
-        top = functools.reduce(jnp.maximum, tops)
-        total = sum(colbuf[it, s, 1:2, :] * jnp.exp2(tops[s] - top) for s in range(nz))
-        return -log_clusters - (top + jnp.log2(total))
-
-    def row_potential(it, col_pot):
+        logs = [colbuf[it, s] for s in range(nz)]
+        top = functools.reduce(jnp.maximum, logs)
+        return -log_clusters - (top + jnp.log2(sum(jnp.exp2(x - top) for x in logs)))
+
+    part = nb // 2
+
+    def row_send(it, h, col_pot):
         def block(b, carry):
-            t = scores[b] + col_pot
+            t = scores[h * part + b] + col_pot
             high = jnp.max(t, axis=1, keepdims=True)
             total = jnp.sum(jnp.exp2(t - high), axis=1, keepdims=True)
-            rowbuf[it, me, pl.ds(b, 1), :] = to_lanes(high)
-            rowbuf[it, me, pl.ds(nb + b, 1), :] = to_lanes(total)
+            rowbuf[it, h, me, pl.ds(b, 1), :] = to_lanes(high + jnp.log2(total))
             return carry
 
-        lax.fori_loop(0, nb, block, 0)
-        mine = rowbuf.at[it, me]
+        lax.fori_loop(0, part, block, 0, unroll=4)
+        mine = rowbuf.at[it, h, me]
         for k in range(1, nb):
-            send(mine, mine, row_ss.at[it, k], row_rs.at[it, me], block_peer(k)[1])
+            send(mine, mine, row_ss.at[it, h, k], row_rs.at[it, h, me], block_peer(k)[1])
+
+    def row_receive(it, h):
         for k in range(1, nb):
             peer, device = block_peer(k)
-            theirs = rowbuf.at[it, peer]
-            remote(theirs, theirs, row_ss.at[it, k], row_rs.at[it, peer], device).wait_recv()
-        high = rowbuf[it, :, 0:nb, :]
-        top = jnp.max(high, axis=0)
-        total = jnp.sum(rowbuf[it, :, nb:, :] * jnp.exp2(high - top[None]), axis=0)
-        rpot[...] = -log_docs - (top + jnp.log2(total))
+            theirs = rowbuf.at[it, h, peer]
+            remote(
+                theirs, theirs, row_ss.at[it, h, k], row_rs.at[it, h, peer], device
+            ).wait_recv()
+        logs = rowbuf[it, h]
+        top = jnp.max(logs, axis=0)
+        total = jnp.sum(jnp.exp2(logs - top[None]), axis=0)
+        rpot[h] = -log_docs - (top + jnp.log2(total))
 
     for it in range(ITERS):
         if it > 0:
-            def again(b, state):
-                return col_update(state, scores[b] + to_sublanes(rpot[pl.ds(b, 1), :]))
-
-            state = lax.fori_loop(
-                0, nb, again,
-                (jnp.full((8, half), -jnp.inf, F32), jnp.zeros((8, half), F32)),
-            )
+            state = (jnp.full((8, half), -jnp.inf, F32), jnp.zeros((8, half), F32))
+            for h in range(2):
+                def again(b, state):
+                    t = scores[h * part + b] + to_sublanes(rpot[h, pl.ds(b, 1), :])
+                    return col_update(state, t)
+
+                row_receive(it - 1, h)
+                state = lax.fori_loop(0, part, again, state, unroll=4)
         col_pot = column_potential(it, state)
-        row_potential(it, col_pot)
-
-    def plan_block(b, mass):
-        t = scores[b] + to_sublanes(rpot[pl.ds(b, 1), :]) + col_pot + log_docs
-        p = jnp.exp2(t)
-        plan[pl.ds(pl.multiple_of(b * rows, rows), rows), :] = p.astype(jnp.bfloat16)
-        return mass + jnp.sum(p.reshape(rows // 8, 8, half), axis=0)
-
-    mass = lax.fori_loop(0, nb, plan_block, jnp.zeros((8, half), F32))
-    sums[...] = lax.dot_general(
-        emb_all[...].reshape(nb * rows, features), plan[...],
-        (((0,), (0,)), ((), ())), preferred_element_type=F32,
-    )
+        for h in range(2):
+            row_send(it, h, col_pot)
+
+    mass = jnp.zeros((8, half), F32)
+    for h in range(2):
+        def plan_block(b, mass):
+            t = scores[h * part + b] + to_sublanes(rpot[h, pl.ds(b, 1), :]) + col_pot + log_docs
+            p = jnp.exp2(t)
+            plan[h, pl.ds(pl.multiple_of(b * rows, rows), rows), :] = p.astype(jnp.bfloat16)
+            return mass + jnp.sum(p.reshape(rows // 8, 8, half), axis=0)
+
+        row_receive(ITERS - 1, h)
+        mass = lax.fori_loop(0, part, plan_block, mass, unroll=4)
+        product = lax.dot_general(
+            emb_all[h * part:(h + 1) * part].reshape(part * rows, features), plan[h],
+            (((0,), (0,)), ((), ())), preferred_element_type=F32,
+        )
+        sums[...] = product if h == 0 else sums[...] + product
     massbuf[d] = jnp.sum(mass, axis=0, keepdims=True)
     far = sorted(range(1, nz), key=lambda k: -min(k, nz - k))
 
@@ -240,28 +261,29 @@
             jax.ShapeDtypeStruct((own_f, own_cols), F32),
             jax.ShapeDtypeStruct((1, own_cols), F32),
         ),
-        in_specs=[pl.BlockSpec(memory_space=pltpu.VMEM)] * 2,
+        in_specs=[pl.BlockSpec(memory_space=pltpu.HBM)] * 2,
         out_specs=(pl.BlockSpec(memory_space=pltpu.VMEM),) * 2,
         scratch_shapes=[
             pltpu.VMEM((nb, rows, features), jnp.bfloat16),
+            pltpu.VMEM((half, features), jnp.bfloat16),
             pltpu.VMEM((nb, rows, half), F32),
-            pltpu.VMEM((nb * rows, half), jnp.bfloat16),
-            pltpu.VMEM((nb, rows), F32),
-            pltpu.VMEM((ITERS, nz, 2, half), F32),
-            pltpu.VMEM((ITERS, nb, 2 * nb, rows), F32),
+            pltpu.VMEM((2, nc * rows, half), jnp.bfloat16),
+            pltpu.VMEM((2, nc, rows), F32),
+            pltpu.VMEM((ITERS, nz, 1, half), F32),
+            pltpu.VMEM((ITERS, 2, nb, nc, rows), F32),
             pltpu.VMEM((nd, 1, half), F32),
             pltpu.VMEM((nd, 1, half), F32),
             pltpu.VMEM((features, half), F32),
             pltpu.VMEM((nz, 2 * own_f, half), F32),
             pltpu.VMEM((2 * own_f, half), F32),
             pltpu.VMEM((own_f, half), F32),
-            dma, dma((nc,)), dma((nb,)), dma((nc,)),
-            dma((ITERS, nz)), dma((ITERS, nz)), dma((ITERS, nb)), dma((ITERS, nb)),
+            dma, dma, dma((nc,)), dma((nb,)), dma((nc,)),
+            dma((ITERS, nz)), dma((ITERS, nz)), dma((ITERS, 2, nb)), dma((ITERS, 2, nb)),
             dma((nd,)), dma((nd,)), dma((nd,)), dma((nd,)),
             dma((nz,)), dma((nz,)), dma, dma,
         ],
         compiler_params=pltpu.CompilerParams(
-            collective_id=0, has_side_effects=True, vmem_limit_bytes=50 * 2**20
+            collective_id=0, has_side_effects=True
         ),
     )(embeddings, centroids)
     return out, mass.reshape(own_cols)

time: 53.4 us -> 49.3 us (0.923)
  Pallas kernels: 49.4 us -> 46.4 us
  local copies, waits for them, and re-layouts: 3.12 us -> 2.17 us
    pallas_call x1, Pallas kernels: 49.4 us -> 46.4 us  [local(): pl.pallas_call(functools.partial(kernel, nd, nc), out_shape=(jax.ShapeDty...]
    unnamed x6 -> x4, local copies, waits for them, and re-layouts: 3.12 us -> 2.17 us
where the time goes in v2:
time: 49.3 us; the launch traced here: 49.2 us
  Pallas kernels  46.4 us (94%)
  local copies, waits for them, and re-layouts  2.17 us (4%)
  between operations  0.65 us (1%)
    pallas_call x1, Pallas kernels, local(): pl.pallas_call(functools.partial(kernel, nd, nc), out_shape=(jax.ShapeDty...  46.4 us
    unnamed x4, local copies, waits for them, and re-layouts  2.17 us

profile of v2, /device:TPU:0, one launch (start us, length us, event | category | flops | bytes accessed | tf_op | source)
XLA Modules:
  0.0 49.2 jit_solution(13911728465356802334)
XLA Ops:
  0.6 46.4 %shard_map.41 = (f32[32,1024]{1,0:T(8,128)}, f32[1,1024]{1,0:T(1,128)}) custom-call(bf16[128,256]{1,0:T(8,128)(2,1)} %emb_ref.1, bf16[1024,256]{1,0:T(8,128)(2,1)} %cent_ref.1), custom_call_target="tpu_custom_call" | custom-call | tf_op jit(solution)/shard_map/pallas_call | solution.py:258
  47.0 0.0 copy-start
  47.0 1.6 %copy.6 = f32[32,1024]{1,0:T(8,128)} copy(f32[32,1024]{1,0:T(8,128)} %get-tuple-element.8) | data formatting | bytes 262144
  48.6 0.0 copy-done
  48.6 0.6 %copy.7 = f32[1024]{0:T(1024)} copy(f32[1024]{0:T(1024)S(1)} %bitcast.1) | data formatting | bytes 8192
Async XLA Ops:
  47.0 1.6 %copy-start = (f32[1,1024]{1,0:T(1,128)S(1)}, f32[1,1024]{1,0:T(1,128)}, u32[]{:S(2)}) copy-start(f32[1,1024]{1,0:T(1,128)} %get-tuple-element.5) | copy-start | bytes 12292
